TPU v7x, 32 devices: a whole 2x2x4 slice. The times are simulated.
32 devices in a mesh: ctx: 8 (over y, x, core), dp: 4 (over z).
Axes of the slice: x: 2, y: 2, z: 4, core: 2. Of those that a mesh axis runs over, the one named last changes fastest.
Arguments:
- ids: int32 [3072], P('ctx'), may hold values from 0 to 511
- embed_table: bfloat16 [512, 4096], P(None, 'dp'), may hold values from -6 to 6
- norm_gain: bfloat16 [4096], P('dp'), may hold values from 0.25 to 1.75
- w_query: bfloat16 [4096, 4096], P('ctx', 'dp'), may hold values from -0.09375 to 0.09375
- w_key: bfloat16 [4096, 4096], P('ctx', 'dp'), may hold values from -0.09375 to 0.09375
- w_value: bfloat16 [4096, 4096], P('ctx', 'dp'), may hold values from -0.09375 to 0.09375
- short_filter: float32 [3, 3, 4096], P(None, None, 'dp'), may hold values from -4 to 4
- pole_rate: float32 [4096, 16], P('dp'), may hold values from 1.6276042e-05 to 0.05
- residue: float32 [4096, 16], P('dp'), may hold values from -2 to 2
- skip_gain: float32 [4096], P('dp'), may hold values from -4 to 4
- w_out: bfloat16 [4096, 4096], P('ctx', 'dp'), may hold values from -0.09375 to 0.09375
Outputs:
- block_out: bfloat16 [3072, 4096], P('ctx', 'dp')
All inputs are finite; a program needn't handle non-finite values.
Results may differ from a plain program's by a relative error of at most 0.0082.
Values may be sent and summed in bfloat16 or wider, within the bound.
A program may use at most 128 MiB of HBM per device.

v0:
```python
import math
import jax
import jax.numpy as jnp
from jax import lax
from jax.sharding import PartitionSpec as P


def shifted(value, axis, steps):
    count = lax.axis_size(axis)
    initial, last = (max(0, -steps), min(count, count - steps))
    return lax.ppermute(value, axis, [(source, source + steps) for source in range(initial, last)])


def entering_2(value, axis, combine, identity):
    peers, index = (lax.axis_size(axis), lax.axis_index(axis))
    everything = jax.tree.map(lambda part: lax.all_gather(part, axis), value)
    start = jax.tree.map(
        lambda part, zero: jnp.broadcast_to(jnp.asarray(zero, part.dtype), part.shape),
        value,
        identity,
    )

    def turn(k, before):
        reached = k < index
        new = combine(before, jax.tree.map(lambda part: part[k], everything))
        return jax.tree.map(lambda a, b: jnp.where(reached, a, b), new, before)

    return lax.fori_loop(0, peers, turn, start)


def shards(
    ids,
    embed_table,
    norm_gain,
    w_query,
    w_key,
    w_value,
    short_filter,
    pole_rate,
    residue,
    skip_gain,
    w_out,
):
    highest = lax.Precision.HIGHEST
    vocab = embed_table.shape[0]
    channels = w_query.shape[1]
    one_hot = (ids[:, None] == jnp.arange(vocab, dtype=jnp.int32)[None, :]).astype(jnp.bfloat16)
    embedded = jnp.dot(one_hot, embed_table, preferred_element_type=jnp.float32).astype(
        jnp.bfloat16
    )
    full_rows, full_gain = (
        lax.all_gather(embedded, "dp", axis=1, tiled=True),
        lax.all_gather(norm_gain, "dp", axis=0, tiled=True),
    )
    floated = full_rows.astype(jnp.float32)
    scale = lax.rsqrt(jnp.mean(floated * floated, axis=1, keepdims=True) + 1e-06)
    normed = (floated * scale * full_gain.astype(jnp.float32)[None, :]).astype(jnp.bfloat16)
    tok_rows = normed.shape[0]

    def add_rows(piece):
        return jnp.dot(normed, piece, preferred_element_type=jnp.float32)

    query_proj = add_rows(lax.all_gather(w_query, "ctx", axis=0, tiled=True))
    key_proj = add_rows(lax.all_gather(w_key, "ctx", axis=0, tiled=True))
    value_proj = add_rows(lax.all_gather(w_value, "ctx", axis=0, tiled=True))
    projected = jnp.concatenate([query_proj, key_proj, value_proj], axis=1).astype(jnp.bfloat16)
    taps = short_filter.shape[0]
    previous = shifted(projected[tok_rows - (taps - 1) :], "ctx", 1)
    extended = jnp.concatenate([previous, projected], axis=0).astype(jnp.float32)
    filt_rows = short_filter.reshape(taps, 3 * channels)
    convolved = jnp.zeros((tok_rows, 3 * channels), jnp.float32)
    for tap in range(taps):
        convolved = (
            convolved
            + filt_rows[tap][None, :] * extended[taps - 1 - tap : taps - 1 - tap + tok_rows]
        )
    query_conv = convolved[:, :channels]
    gated = convolved[:, channels : 2 * channels] * convolved[:, 2 * channels :]
    sub_len = math.gcd(tok_rows, 64)
    blocks = tok_rows // sub_len
    lag_index = jnp.arange(sub_len, dtype=jnp.int32)
    lags = lag_index.astype(jnp.float32)
    strength = residue * jnp.sqrt(2.0 * pole_rate)
    kernel = jnp.einsum(
        "lck,ck->lc", jnp.exp(-pole_rate[None] * lags[:, None, None]), strength, precision=highest
    )
    offsets = lag_index[:, None] - lag_index[None, :]
    toeplitz = jnp.where((offsets >= 0)[:, :, None], kernel[jnp.maximum(offsets, 0)], 0.0)
    pieces = gated.reshape(blocks, sub_len, channels)
    inside = jnp.einsum("tsc,bsc->btc", toeplitz, pieces, precision=highest)
    tail_decay = jnp.exp(-pole_rate[None] * (sub_len - 1.0 - lags)[:, None, None])
    block_ends = jnp.einsum("sck,bsc->bck", tail_decay, pieces, precision=highest)
    step_decay = jnp.exp(-pole_rate * float(sub_len))

    def advance(state, block_end):
        return (step_decay * state + block_end, state)

    device_end, entering = lax.scan(advance, jnp.zeros_like(step_decay), block_ends)
    device_decay = jnp.exp(-pole_rate * float(tok_rows))

    def combine(earlier, later):
        return (earlier[0] * later[0], later[0] * earlier[1] + later[1])

    decay_total, incoming = entering_2(
        (device_decay, device_end),
        "ctx",
        combine,
        (jnp.ones_like(device_decay), jnp.zeros_like(device_end)),
    )
    block_pos = jnp.arange(blocks, dtype=jnp.float32) * float(sub_len)
    states_in = entering + jnp.exp(-pole_rate[None] * block_pos[:, None, None]) * incoming[None]
    lead = jnp.exp(-pole_rate[None] * (lags + 1.0)[:, None, None]) * strength[None]
    carried = jnp.einsum("tck,bck->btc", lead, states_in, precision=highest)
    long_conv = (inside + carried).reshape(tok_rows, channels) + skip_gain[None, :] * gated
    mixed = (query_conv * long_conv).astype(jnp.bfloat16)
    all_mixed = lax.all_gather(mixed, "dp", axis=1, tiled=True)
    output = jnp.dot(
        all_mixed,
        lax.all_gather(w_out, "ctx", axis=0, tiled=True),
        preferred_element_type=jnp.float32,
    )
    return (embedded.astype(jnp.float32) + output).astype(jnp.bfloat16)


def solution(mesh):
    placed = (
        P("ctx"),
        P(None, "dp"),
        P("dp"),
        P("ctx", "dp"),
        P("ctx", "dp"),
        P("ctx", "dp"),
        P(None, None, "dp"),
        P("dp", None),
        P("dp", None),
        P("dp"),
        P("ctx", "dp"),
    )
    return jax.shard_map(
        shards, mesh=mesh, in_specs=placed, out_specs=P("ctx", "dp"), check_vma=False
    )
```

profile of v0, /device:TPU:0, one launch (start us, length us, event | category | flops | bytes accessed | tf_op | source)
XLA Modules:
  0.0 511.5 jit_solution(16965274444478616923)
XLA Ops:
  6.6 1.2 copy-done
  7.8 2.2 convolution_convert_fusion.3
  13.3 12.5 %multiply_reduce_fusion = f32[1024,64]{1,0:T(8,128)} fusion(f32[1024,16]{1,0:T(8,128)S(1)} %copy.47, f32[64]{0:T(128)S(1)} %iota_convert_fusion, f32[1024,16]{1,0:T(8,128)S(1)} %copy.30), kind=kLoop, calls=%fused_computation.14 | loop fusion | flops 3080192 | bytes 393472
  25.9 14.8 %all_gather.34 = bf16[4096]{0:T(1024)(128)(2,1)S(1)} all-gather(bf16[1024]{0:T(1024)(128)(2,1)S(1)} %copy-done.12), channel_id=1, replica_groups=mesh['ctx'=8,'dp'=4] {'dp'}, dimensions={0}, use_global_device_ids=true | all-gather | bytes 10240 | tf_op jit(solution)/shard_map/all_gather | solution.py:53
  40.7 10.9 %all-gather = f32[8192,16]{0,1:T(8,128)} all-gather(f32[1024,16]{0,1:T(8,128)S(1)} %get-tuple-element.213), channel_id=2, replica_groups=mesh['ctx'=8,'dp'=4] {'ctx'}, dimensions={0}, use_global_device_ids=true | all-gather | bytes 589824 | tf_op jit(solution)/shard_map/all_gather | solution.py:16
  51.6 24.7 %all-gather.9.cloned.1.call-done = bf16[384,4096]{1,0:T(8,128)(2,1)} async-done(((bf16[384,1024]{1,0:T(8,128)(2,1)}), bf16[384,4096]{1,0:T(8,128)(2,1)}) %all-gather.9.cloned.1.call-update) | async-done | bytes 3145744 | tf_op jit(solution)/shard_map/all_gather | solution.py:52
  76.3 2.6 fusion.14
  78.9 52.2 %all-gather.15.cloned.1.call-done = bf16[4096,1024]{1,0:T(8,128)(2,1)} async-done(((bf16[512,1024]{1,0:T(8,128)(2,1)}), bf16[4096,1024]{1,0:T(8,128)(2,1)}) %all-gather.15.cloned.1.call-update) | async-done | bytes 8388624 | tf_op jit(solution)/shard_map/all_gather | solution.py:65
  131.2 7.8 %convolution_convert_fusion = bf16[384,1024]{1,0:T(8,128)(2,1)S(1)} fusion(bf16[4096,1024]{1,0:T(8,128)(2,1)} %all-gather.15.cloned.1.call-done, bf16[384,4096]{1,0:T(8,128)(2,1)} %all-gather.9.cloned.1.call-done, f32[4096]{0:T(1024)S(1)} %convert_element_type.46, f32[384]{0:T(512)S(1)} %add_rsqrt_fusion), kind=kOutput, calls=%fused_computation.45 | convolution fusion | flops 3227910144 | bytes 12338688 | tf_op jit(solution)/shard_map/dot_general | solution.py:61
  139.0 48.4 %all-gather.13.cloned.1.call-done = bf16[4096,1024]{1,0:T(8,128)(2,1)} async-done(((bf16[512,1024]{1,0:T(8,128)(2,1)}), bf16[4096,1024]{1,0:T(8,128)(2,1)}) %all-gather.13.cloned.1.call-update) | async-done | bytes 8388624 | tf_op jit(solution)/shard_map/all_gather | solution.py:64
  187.3 7.8 %convolution_convert_fusion.1 = bf16[384,1024]{1,0:T(8,128)(2,1)S(1)} fusion(bf16[4096,1024]{1,0:T(8,128)(2,1)} %all-gather.13.cloned.1.call-done, bf16[384,4096]{1,0:T(8,128)(2,1)} %all-gather.9.cloned.1.call-done, f32[4096]{0:T(1024)S(1)} %convert_element_type.46, f32[384]{0:T(512)S(1)} %add_rsqrt_fusion), kind=kOutput, calls=%fused_computation.46 | convolution fusion | flops 3227910144 | bytes 12338688 | tf_op jit(solution)/shard_map/dot_general | solution.py:61
  195.1 48.2 %all-gather.11.cloned.1.call-done = bf16[4096,1024]{1,0:T(8,128)(2,1)} async-done(((bf16[512,1024]{1,0:T(8,128)(2,1)}), bf16[4096,1024]{1,0:T(8,128)(2,1)}) %all-gather.11.cloned.1.call-update) | async-done | bytes 8388624 | tf_op jit(solution)/shard_map/all_gather | solution.py:63
  243.4 7.8 %convolution_convert_fusion.2 = bf16[384,1024]{1,0:T(8,128)(2,1)S(1)} fusion(bf16[4096,1024]{1,0:T(8,128)(2,1)} %all-gather.11.cloned.1.call-done, bf16[384,4096]{1,0:T(8,128)(2,1)} %all-gather.9.cloned.1.call-done, f32[4096]{0:T(1024)S(1)} %convert_element_type.46, f32[384]{0:T(512)S(1)} %add_rsqrt_fusion), kind=kOutput, calls=%fused_computation.47 | convolution fusion | flops 3227910144 | bytes 12338688 | tf_op jit(solution)/shard_map/dot_general | solution.py:61
  251.2 2.2 collective-permute-start
  253.5 1.2 copy.44
  254.7 18.9 %gather_fusion = f32[4096,1024]{1,0:T(8,128)} fusion(f32[64,1024]{1,0:T(8,128)S(1)} %bitcast.57, s32[4096]{0:T(1024)S(1)} %broadcast_clamp_fusion), kind=kCustom, calls=%fused_computation | custom fusion | bytes 33570816 | tf_op jit(solution)/shard_map/gather | solution.py:88
  273.6 30.7 %copy.31 = f32[64,64,1024]{1,0,2:T(8,128)} copy(f32[64,64,1024]{2,1,0:T(8,128)} %bitcast.58) | data formatting | bytes 33554432 | tf_op jit(solution)/shard_map/gather | solution.py:88
  304.3 2.1 copy.48
  307.2 1.4 fusion.17
  308.6 2.2 copy-done.2
  311.1 2.7 copy.32
  313.8 16.9 %fusion.24 = f32[6,1024,16]{2,0,1:T(8,128)} fusion(f32[6,64,1024]{1,0,2:T(8,128)} %copy.32, f32[64]{0:T(128)S(1)} %broadcast_subtract_fusion, f32[1024,16]{1,0:T(8,128)S(1)} %copy.30), kind=kOutput, calls=%fused_computation.39 | convolution fusion | flops 76546048 | bytes 2031872 | tf_op jit(solution)/shard_map/sck,bsc->bck/dot_general | solution.py:92
  330.7 2.7 copy.34
  333.8 10.3 %all-gather.1 = f32[8192,16]{0,1:T(8,128)S(1)} all-gather(f32[1024,16]{0,1:T(8,128)S(1)} %get-tuple-element.128), channel_id=3, replica_groups=mesh['ctx'=8,'dp'=4] {'ctx'}, dimensions={0}, use_global_device_ids=true | all-gather | bytes 589824 | tf_op jit(solution)/shard_map/all_gather | solution.py:16
  344.3 9.8 %while.28 = (s32[]{:T(128)}, f32[1024,16]{0,1:T(8,128)S(1)}, s32[]{:T(128)}, f32[8,1024,16]{1,0,2:T(8,128)}, f32[8,1024,16]{1,0,2:T(8,128)S(1)}, /*index=5*/s32[]{:T(128)}, s32[]{:T(128)}) while((s32[]{:T(128)}, f32[1024,16]{0,1:T(8,128)S(1)}, s32[]{:T(128)}, f32[8,1024,16]{1,0,2:T(8,128)}, f32[8,1024,16]{1,0,2:T(8,128)S(1)}, ...), condition=%wide.region_4.5_spmd.clone, body=%wide.region_3.4_spmd.clone.sunk | while | flops 65540 | bytes 524397 | solution.py:28
  354.2 2.7 copy.38
  356.9 56.2 %fusion.3 = f32[1024,6,64]{2,1,0:T(8,128)S(1)} fusion(f32[6,64,1024]{1,0,2:T(8,128)} %copy.32, f32[64,64,1024]{1,0,2:T(8,128)} %copy.31, pred[64,64]{1,0:T(8,128)(4,1)S(1)} %subtract_compare_fusion), kind=kOutput, calls=%fused_computation.10 | convolution fusion | flops 306184192 | bytes 19927040 | tf_op jit(solution)/shard_map/tsc,bsc->btc/dot_general | solution.py:90
  413.2 12.3 %add_bitcast_fusion = f32[6,64,1024]{1,0,2:T(8,128)} fusion(f32[1024,6,64]{2,1,0:T(8,128)S(1)} %fusion.3, f32[6,1024,16]{2,0,1:T(8,128)S(1)} %copy-done.3, f32[1024,16]{1,0:T(8,128)S(1)} %copy-done.6, f32[64]{0:T(128)S(1)} %broadcast_add_fusion, f32[1024,16]{1,0:T(8,128)S(1)} %copy.30), kind=kOutput, calls=%fused_computation.32 | convolution fusion | flops 77987840 | bytes 3670272 | tf_op jit(solution)/shard_map/tck,bck->btc/dot_general | solution.py:113
  425.5 2.7 copy.39
  428.2 3.9 fusion.29
  432.2 63.5 %all-gather.17.cloned.1.call-done = bf16[384,4096]{1,0:T(8,128)(2,1)} async-done(((bf16[384,1024]{1,0:T(8,128)(2,1)}), bf16[384,4096]{1,0:T(8,128)(2,1)}) %all-gather.17.cloned.1.call-update) | async-done | bytes 3145744 | tf_op jit(solution)/shard_map/all_gather | solution.py:116
  495.8 8.7 %add_convert_fusion = bf16[384,1024]{1,0:T(8,128)(2,1)} fusion(bf16[384,1024]{1,0:T(8,128)(2,1)S(1)} %copy-done.4, bf16[384,4096]{1,0:T(8,128)(2,1)} %all-gather.17.cloned.1.call-done, bf16[4096,1024]{1,0:T(8,128)(2,1)} %all-gather.19.cloned.1.call-done), kind=kOutput, calls=%fused_computation.44 | convolution fusion | flops 3222405120 | bytes 13107200 | tf_op jit(solution)/shard_map/dot_general | solution.py:117
  (92 shorter events, 14.9 us)
Async XLA Ops:
  6.5 1.2 copy-start
  6.5 6.2 %copy-start.10 = (f32[3,3,1024]{2,1,0:T(4,128)S(1)}, f32[3,3,1024]{2,1,0:T(4,128)}, u32[]{:S(2)}) copy-start(f32[3,3,1024]{2,1,0:T(4,128)} %param.21) | copy-start | bytes 110596
  6.5 6.2 %copy-start.8 = (f32[1024,16]{0,1:T(8,128)S(1)}, f32[1024,16]{0,1:T(8,128)}, u32[]{:S(2)}) copy-start(f32[1024,16]{0,1:T(8,128)} %param.22) | copy-start | bytes 196612
  6.5 6.2 %copy-start.9 = (f32[1024,16]{0,1:T(8,128)S(1)}, f32[1024,16]{0,1:T(8,128)}, u32[]{:S(2)}) copy-start(f32[1024,16]{0,1:T(8,128)} %param.23) | copy-start | bytes 196612
  6.5 69.8 %all-gather.9.cloned.1.call-start = ((), (), s32[]{:S(2)}) async-start(), calls=%async_computation | async-start | bytes 3932160 | tf_op jit(solution)/shard_map/all_gather | solution.py:52
  9.9 15.9 %copy-start.12 = (bf16[1024]{0:T(1024)(128)(2,1)S(1)}, bf16[1024]{0:T(1024)(128)(2,1)}, u32[]{:S(2)}) copy-start(bf16[1024]{0:T(1024)(128)(2,1)} %param.17) | copy-start | bytes 6148
  10.0 121.2 %all-gather.15.cloned.1.call-start = ((), (), s32[]{:S(2)}) async-start(), calls=%async_computation.3 | async-start | bytes 9437184 | tf_op jit(solution)/shard_map/all_gather | solution.py:65
  10.7 176.6 %all-gather.13.cloned.1.call-start = ((), (), s32[]{:S(2)}) async-start(), calls=%async_computation.2 | async-start | bytes 9437184 | tf_op jit(solution)/shard_map/all_gather | solution.py:64
  11.5 231.9 %all-gather.11.cloned.1.call-start = ((), (), s32[]{:S(2)}) async-start(), calls=%async_computation.1 | async-start | bytes 9437184 | tf_op jit(solution)/shard_map/all_gather | solution.py:63
  12.0 420.2 %all-gather.19.cloned.1.call-start = ((), (), s32[]{:S(2)}) async-start(), calls=%async_computation.5 | async-start | bytes 9437184 | tf_op jit(solution)/shard_map/all_gather | solution.py:119
  12.6 483.1 %all-gather.17.cloned.1.call-start = ((), (), s32[]{:S(2)}) async-start(), calls=%async_computation.4 | async-start | bytes 3932160 | tf_op jit(solution)/shard_map/all_gather | solution.py:116
  13.0 65.9 %copy-start.5 = (f32[1024,16]{1,0:T(8,128)}, f32[1024,16]{1,0:T(8,128)S(1)}, u32[]{:S(2)}) copy-start(f32[1024,16]{1,0:T(8,128)S(1)} %copy.47) | copy-start | bytes 196612
  251.2 55.3 %collective-permute-start = (bf16[2,3072]{1,0:T(2,128)(2,1)S(1)}, bf16[2,3072]{1,0:T(2,128)(2,1)S(1)}, u32[]{:S(2)}, u32[]{:S(2)}) collective-permute-start(bf16[2,3072]{1,0:T(2,128)(2,1)S(1)} %pad_maximum_fusion), channel_id=1, source_target_pairs={{0,4},{4,8},{8,12},{12,16},{16,20},{20,24},{24,28},{1,5},{5,9},{9,... | collective-permute-start | bytes 36872 | tf_op jit(solution)/shard_map/ppermute | solution.py:11
  308.6 2.2 copy-start.2
  313.8 19.5 %copy-start.7 = (f32[6,1024,16]{1,2,0:T(8,128)S(1)}, f32[6,1024,16]{1,2,0:T(8,128)}, u32[]{:S(2)}) copy-start(f32[6,1024,16]{1,2,0:T(8,128)} %custom-call.4) | copy-start | bytes 1179652
  356.9 56.2 %copy-start.3 = (f32[6,1024,16]{2,0,1:T(8,128)S(1)}, f32[6,1024,16]{2,0,1:T(8,128)}, u32[]{:S(2)}) copy-start(f32[6,1024,16]{2,0,1:T(8,128)} %copy.38) | copy-start | bytes 1179652
  356.9 56.2 %copy-start.6 = (f32[1024,16]{1,0:T(8,128)S(1)}, f32[1024,16]{1,0:T(8,128)}, u32[]{:S(2)}) copy-start(f32[1024,16]{1,0:T(8,128)} %copy-done.5) | copy-start | bytes 196612
  425.5 2.7 copy-start.11
  428.2 67.5 %copy-start.4 = (bf16[384,1024]{1,0:T(8,128)(2,1)S(1)}, bf16[384,1024]{1,0:T(8,128)(2,1)}, u32[]{:S(2)}) copy-start(bf16[384,1024]{1,0:T(8,128)(2,1)} %convolution_convert_fusion.3) | copy-start | bytes 2359300
  495.8 8.7 %copy-start.1 = (bf16[512,1024]{1,0:T(8,128)(2,1)S(1)}, bf16[512,1024]{1,0:T(8,128)(2,1)}, u32[]{:S(2)}) copy-start(bf16[512,1024]{1,0:T(8,128)(2,1)} %param.16) | copy-start | bytes 3145732
Sparse Core Ops, SparseCore 0:
  10.1 66.2 all-gather.8
  78.2 52.8 all-gather.14
  133.0 54.2 all-gather.12
  189.1 54.2 all-gather.10
  245.1 54.2 all-gather.18
  432.3 63.4 all-gather.16
where the time goes:
time: 521 us; the launch traced here: 512 us
  waiting for transfers between devices  240 us (46%)
  matrix products  120 us (23%)
  local copies, waits for them, and re-layouts  77.3 us (15%)
  blocking collectives  36 us (7%)
  other arithmetic  22.2 us (4%)
  between operations  14 us (3%)
    all_gather x1, waiting for transfers between devices, shards(): all_mixed = lax.all_gather(mixed, 'dp', axis=1, tiled=True)  63.5 us
    dot_general x1, matrix products, shards(): inside = jnp.einsum('tsc,bsc->btc', toeplitz, pieces, precision=highest)  56.2 us
    all_gather x1, waiting for transfers between devices, shards(): value_proj = add_rows(lax.all_gather(w_value, 'ctx', axis=0, tiled=True))  52.2 us
    gather x2, local copies, waits for them, and re-layouts, shards(): kernel[jnp.maximum(offsets, 0)]  49.6 us
    all_gather x1, waiting for transfers between devices, shards(): key_proj = add_rows(lax.all_gather(w_key, 'ctx', axis=0, tiled=True))  48.4 us
    all_gather x1, waiting for transfers between devices, shards(): query_proj = add_rows(lax.all_gather(w_query, 'ctx', axis=0, tiled=True))  48.2 us
    all_gather x1, waiting for transfers between devices, shards(): lax.all_gather(embedded, 'dp', axis=1, tiled=True)  24.7 us
    dot_general x3, matrix products, add_rows(): return jnp.dot(normed, piece, preferred_element_type=jnp.float32)  23.4 us
  transfers between devices with their start and end apart: 7, of which 5 were waited for; matrix products, arithmetic and copies ran while one was open for 40% of the time, Pallas kernels for 0%

commit v1 on v0

--- a/solution.py
+++ b/solution.py
@@ -3,6 +3,19 @@
 import jax.numpy as jnp
 from jax import lax
 from jax.sharding import PartitionSpec as P
+
+
+def collect(value, axis, dim):
+    size, place, rows = (lax.axis_size(axis), lax.axis_index(axis), value.shape[dim])
+    right = [(i, (i + 1) % size) for i in range(size)]
+    out = jnp.zeros((*value.shape[:dim], size * rows, *value.shape[dim + 1 :]), value.dtype)
+    carried = value
+    for step in range(size):
+        holder = (place - step) % size
+        out = lax.dynamic_update_slice_in_dim(out, carried, holder * rows, axis=dim)
+        if step < size - 1:
+            carried = lax.ppermute(carried, axis, right)
+    return out
 
 
 def shifted(value, axis, steps):
@@ -60,7 +73,7 @@
     def add_rows(piece):
         return jnp.dot(normed, piece, preferred_element_type=jnp.float32)
 
-    query_proj = add_rows(lax.all_gather(w_query, "ctx", axis=0, tiled=True))
+    query_proj = add_rows(collect(w_query, "ctx", 0))
     key_proj = add_rows(lax.all_gather(w_key, "ctx", axis=0, tiled=True))
     value_proj = add_rows(lax.all_gather(w_value, "ctx", axis=0, tiled=True))
     projected = jnp.concatenate([query_proj, key_proj, value_proj], axis=1).astype(jnp.bfloat16)

time: 521 us -> 477 us (0.916)
  waiting for transfers between devices: 240 us -> 160 us
  local copies, waits for them, and re-layouts: 77.3 us -> 97.3 us
  blocking collectives: 36 us -> 50.1 us
    ppermute x0 -> x7, waiting for transfers between devices: none -> 64.6 us  [collect(): carried = lax.ppermute(carried, axis, right)]
    all_gather x1, waiting for transfers between devices: 52.2 us -> 0.02 us  [shards(): value_proj = add_rows(lax.all_gather(w_value, 'ctx', axis=0, tiled=True))]
    all_gather x1 -> x0, waiting for transfers between devices: 48.2 us -> none  [shards(): query_proj = add_rows(lax.all_gather(w_query, 'ctx', axis=0, tiled=True))]
    all_gather x1, waiting for transfers between devices: 24.7 us -> 0.01 us  [shards(): lax.all_gather(embedded, 'dp', axis=1, tiled=True)]
    all_gather x1, waiting for transfers between devices: 48.4 us -> 30.5 us  [shards(): key_proj = add_rows(lax.all_gather(w_key, 'ctx', axis=0, tiled=True))]
    all_gather x2, blocking collectives: 21.1 us -> 37.6 us  [entering_2(): everything = jax.tree.map(lambda part: lax.all_gather(part, axis), value)]
    dynamic_update_slice x0 -> x8, local copies, waits for them, and re-layouts: none -> 15 us  [collect(): out = lax.dynamic_update_slice_in_dim(out, carried, holder * rows, axis=dim)]
  transfers between devices with their start and end apart: 7 -> 13, of which waited for: 5 -> 7; matrix products, arithmetic and copies ran while one was open for 40% -> 48% of each run, Pallas kernels for 0% -> 0%
where the time goes in v1:
time: 477 us; the launch traced here: 471 us
  waiting for transfers between devices  160 us (34%)
  matrix products  118 us (25%)
  local copies, waits for them, and re-layouts  97.3 us (20%)
  blocking collectives  50.1 us (11%)
  other arithmetic  25.8 us (5%)
  between operations  13.9 us (3%)
  starting transfers between devices  5.41 us (1%)
    ppermute x7, waiting for transfers between devices, collect(): carried = lax.ppermute(carried, axis, right)  64.6 us
    all_gather x1, waiting for transfers between devices, shards(): all_mixed = lax.all_gather(mixed, 'dp', axis=1, tiled=True)  63.6 us
    dot_general x1, matrix products, shards(): inside = jnp.einsum('tsc,bsc->btc', toeplitz, pieces, precision=highest)  56.2 us
    gather x2, local copies, waits for them, and re-layouts, shards(): kernel[jnp.maximum(offsets, 0)]  49.5 us
    all_gather x2, blocking collectives, entering_2(): everything = jax.tree.map(lambda part: lax.all_gather(part, axis), value)  37.6 us
    all_gather x1, waiting for transfers between devices, shards(): key_proj = add_rows(lax.all_gather(w_key, 'ctx', axis=0, tiled=True))  30.5 us
    dot_general x3, matrix products, add_rows(): return jnp.dot(normed, piece, preferred_element_type=jnp.float32)  21.7 us
    dot_general x1, matrix products, shards(): jnp.einsum('sck,bsc->bck', tail_decay, pieces, precision=highest)  16.8 us
  transfers between devices with their start and end apart: 13, of which 7 were waited for; matrix products, arithmetic and copies ran while one was open for 48% of the time, Pallas kernels for 0%

profile of v1, /device:TPU:0, one launch (start us, length us, event | category | flops | bytes accessed | tf_op | source)
XLA Modules:
  0.0 471.0 jit_solution(14489906686665083404)
XLA Ops:
  12.1 15.6 %collective-permute-done = bf16[512,1024]{1,0:T(8,128)(2,1)S(1)} collective-permute-done((bf16[512,1024]{1,0:T(8,128)(2,1)}, bf16[512,1024]{1,0:T(8,128)(2,1)S(1)}, u32[]{:S(2)}, u32[]{:S(2)}) %collective-permute-start) | collective-permute-done | bytes 1048608 | tf_op jit(solution)/shard_map/ppermute | solution.py:17
  27.6 15.1 %collective-permute-done.1 = bf16[512,1024]{1,0:T(8,128)(2,1)S(1)} collective-permute-done((bf16[512,1024]{1,0:T(8,128)(2,1)S(1)}, bf16[512,1024]{1,0:T(8,128)(2,1)S(1)}, u32[]{:S(2)}, u32[]{:S(2)}) %collective-permute-start.1) | collective-permute-done | bytes 1048608 | tf_op jit(solution)/shard_map/ppermute | solution.py:17
  42.8 15.1 %collective-permute-done.2 = bf16[512,1024]{1,0:T(8,128)(2,1)S(1)} collective-permute-done((bf16[512,1024]{1,0:T(8,128)(2,1)S(1)}, bf16[512,1024]{1,0:T(8,128)(2,1)S(1)}, u32[]{:S(2)}, u32[]{:S(2)}) %collective-permute-start.2) | collective-permute-done | bytes 1048608 | tf_op jit(solution)/shard_map/ppermute | solution.py:17
  58.2 14.9 %collective-permute-done.3 = bf16[512,1024]{1,0:T(8,128)(2,1)} collective-permute-done((bf16[512,1024]{1,0:T(8,128)(2,1)S(1)}, bf16[512,1024]{1,0:T(8,128)(2,1)}, u32[]{:S(2)}, u32[]{:S(2)}) %collective-permute-start.3) | collective-permute-done | bytes 1048608 | tf_op jit(solution)/shard_map/ppermute | solution.py:17
  73.2 27.4 %all-gather = f32[8192,16]{0,1:T(8,128)} all-gather(f32[1024,16]{0,1:T(8,128)S(1)} %get-tuple-element.213), channel_id=2, replica_groups=mesh['ctx'=8,'dp'=4] {'ctx'}, dimensions={0}, use_global_device_ids=true | all-gather | bytes 589824 | tf_op jit(solution)/shard_map/all_gather | solution.py:29
  100.6 4.3 broadcast_in_dim.15
  106.2 12.5 %all_gather.31 = bf16[4096]{0:T(1024)(128)(2,1)S(1)} all-gather(bf16[1024]{0:T(1024)(128)(2,1)S(1)} %copy-done.15), channel_id=1, replica_groups=mesh['ctx'=8,'dp'=4] {'dp'}, dimensions={0}, use_global_device_ids=true | all-gather | bytes 10240 | tf_op jit(solution)/shard_map/all_gather | solution.py:66
  120.0 16.1 %multiply_reduce_fusion = f32[1024,64]{1,0:T(8,128)} fusion(f32[1024,16]{1,0:T(8,128)} %copy.47, f32[64]{0:T(128)S(1)} %iota_convert_fusion, f32[1024,16]{1,0:T(8,128)S(1)} %copy.30), kind=kLoop, calls=%fused_computation.14 | loop fusion | flops 3080192 | bytes 393472
  136.1 2.4 constant_dynamic-update-slice_fusion.6
  140.8 2.3 collective-permute-start.6
  144.1 2.4 constant_dynamic-update-slice_fusion.3
  146.6 2.7 fusion.14
  152.7 3.8 collective-permute-done.6
  156.5 2.5 constant_dynamic-update-slice_fusion
  159.0 6.1 %convolution_convert_fusion.2 = bf16[384,1024]{1,0:T(8,128)(2,1)S(1)} fusion(bf16[4096,1024]{1,0:T(8,128)(2,1)} %constant_dynamic-update-slice_fusion, bf16[384,4096]{1,0:T(8,128)(2,1)S(1)} %copy-done.4, f32[4096]{0:T(1024)S(1)} %convert_element_type.46, f32[384]{0:T(512)S(1)} %add_rsqrt_fusion), kind=kOutput, calls=%fused_computation.47 | convolution fusion | flops 3227910144 | bytes 12338688 | tf_op jit(solution)/shard_map/dot_general | solution.py:74
  165.1 7.8 %convolution_convert_fusion = bf16[384,1024]{1,0:T(8,128)(2,1)S(1)} fusion(bf16[4096,1024]{1,0:T(8,128)(2,1)} %all-gather.12.cloned.1.call-done, bf16[384,4096]{1,0:T(8,128)(2,1)} %all-gather.8.cloned.1.call-done, f32[4096]{0:T(1024)S(1)} %convert_element_type.46, f32[384]{0:T(512)S(1)} %add_rsqrt_fusion), kind=kOutput, calls=%fused_computation.45 | convolution fusion | flops 3227910144 | bytes 12338688 | tf_op jit(solution)/shard_map/dot_general | solution.py:74
  172.9 30.5 %all-gather.10.cloned.1.call-done = bf16[4096,1024]{1,0:T(8,128)(2,1)} async-done(((bf16[512,1024]{1,0:T(8,128)(2,1)}), bf16[4096,1024]{1,0:T(8,128)(2,1)}) %all-gather.10.cloned.1.call-update) | async-done | bytes 8388624 | tf_op jit(solution)/shard_map/all_gather | solution.py:77
  203.4 7.8 %convolution_convert_fusion.1 = bf16[384,1024]{1,0:T(8,128)(2,1)S(1)} fusion(bf16[4096,1024]{1,0:T(8,128)(2,1)} %all-gather.10.cloned.1.call-done, bf16[384,4096]{1,0:T(8,128)(2,1)} %all-gather.8.cloned.1.call-done, f32[4096]{0:T(1024)S(1)} %convert_element_type.46, f32[384]{0:T(512)S(1)} %add_rsqrt_fusion), kind=kOutput, calls=%fused_computation.46 | convolution fusion | flops 3227910144 | bytes 12338688 | tf_op jit(solution)/shard_map/dot_general | solution.py:74
  214.7 18.7 %gather_fusion = f32[4096,1024]{1,0:T(8,128)} fusion(f32[64,1024]{1,0:T(8,128)S(1)} %bitcast.57, s32[4096]{0:T(1024)S(1)} %broadcast_clamp_fusion), kind=kCustom, calls=%fused_computation | custom fusion | bytes 33570816 | tf_op jit(solution)/shard_map/gather | solution.py:101
  233.4 30.8 %copy.31 = f32[64,64,1024]{1,0,2:T(8,128)} copy(f32[64,64,1024]{2,1,0:T(8,128)} %bitcast.58) | data formatting | bytes 33554432 | tf_op jit(solution)/shard_map/gather | solution.py:101
  271.0 2.7 copy.32
  273.7 16.8 %fusion.24 = f32[6,1024,16]{2,0,1:T(8,128)} fusion(f32[6,64,1024]{1,0,2:T(8,128)} %copy.32, f32[64]{0:T(128)S(1)} %broadcast_subtract_fusion, f32[1024,16]{1,0:T(8,128)S(1)} %copy.30), kind=kOutput, calls=%fused_computation.39 | convolution fusion | flops 76546048 | bytes 2031872 | tf_op jit(solution)/shard_map/sck,bsc->bck/dot_general | solution.py:105
  290.5 2.7 copy.34
  293.6 10.2 %all-gather.1 = f32[8192,16]{0,1:T(8,128)S(1)} all-gather(f32[1024,16]{0,1:T(8,128)S(1)} %get-tuple-element.128), channel_id=3, replica_groups=mesh['ctx'=8,'dp'=4] {'ctx'}, dimensions={0}, use_global_device_ids=true | all-gather | bytes 589824 | tf_op jit(solution)/shard_map/all_gather | solution.py:29
  304.1 9.8 %while.28 = (s32[]{:T(128)}, f32[1024,16]{0,1:T(8,128)S(1)}, s32[]{:T(128)}, f32[8,1024,16]{1,0,2:T(8,128)}, f32[8,1024,16]{1,0,2:T(8,128)S(1)}, /*index=5*/s32[]{:T(128)}, s32[]{:T(128)}) while((s32[]{:T(128)}, f32[1024,16]{0,1:T(8,128)S(1)}, s32[]{:T(128)}, f32[8,1024,16]{1,0,2:T(8,128)}, f32[8,1024,16]{1,0,2:T(8,128)S(1)}, ...), condition=%wide.region_4.5_spmd.clone, body=%wide.region_3.4_spmd.clone.sunk | while | flops 65540 | bytes 524397 | solution.py:41
  314.0 2.7 copy.38
  316.7 56.2 %fusion.3 = f32[1024,6,64]{2,1,0:T(8,128)S(1)} fusion(f32[6,64,1024]{1,0,2:T(8,128)} %copy.32, f32[64,64,1024]{1,0,2:T(8,128)} %copy.31, pred[64,64]{1,0:T(8,128)(4,1)S(1)} %subtract_compare_fusion), kind=kOutput, calls=%fused_computation.10 | convolution fusion | flops 306184192 | bytes 19927040 | tf_op jit(solution)/shard_map/tsc,bsc->btc/dot_general | solution.py:103
  372.9 12.4 %add_bitcast_fusion = f32[6,64,1024]{1,0,2:T(8,128)} fusion(f32[1024,6,64]{2,1,0:T(8,128)S(1)} %fusion.3, f32[6,1024,16]{2,0,1:T(8,128)S(1)} %copy-done.3, f32[1024,16]{1,0:T(8,128)S(1)} %copy-done.9, f32[64]{0:T(128)S(1)} %broadcast_add_fusion, f32[1024,16]{1,0:T(8,128)S(1)} %copy.30), kind=kOutput, calls=%fused_computation.32 | convolution fusion | flops 77987840 | bytes 3670272 | tf_op jit(solution)/shard_map/tck,bck->btc/dot_general | solution.py:126
  385.3 2.8 copy.39
  388.1 3.8 fusion.29
  392.0 63.6 %all-gather.14.cloned.1.call-done = bf16[384,4096]{1,0:T(8,128)(2,1)} async-done(((bf16[384,1024]{1,0:T(8,128)(2,1)}), bf16[384,4096]{1,0:T(8,128)(2,1)}) %all-gather.14.cloned.1.call-update) | async-done | bytes 3145744 | tf_op jit(solution)/shard_map/all_gather | solution.py:129
  455.5 8.7 %add_convert_fusion = bf16[384,1024]{1,0:T(8,128)(2,1)} fusion(bf16[384,1024]{1,0:T(8,128)(2,1)S(1)} %copy-done.8, bf16[384,4096]{1,0:T(8,128)(2,1)} %all-gather.14.cloned.1.call-done, bf16[4096,1024]{1,0:T(8,128)(2,1)} %all-gather.16.cloned.1.call-done), kind=kOutput, calls=%fused_computation.44 | convolution fusion | flops 3222405120 | bytes 13107200 | tf_op jit(solution)/shard_map/dot_general | solution.py:130
  (118 shorter events, 35.6 us)
Async XLA Ops:
  6.5 1.2 copy-start
  6.5 66.6 %copy-start.11 = (f32[1024,16]{0,1:T(8,128)S(1)}, f32[1024,16]{0,1:T(8,128)}, u32[]{:S(2)}) copy-start(f32[1024,16]{0,1:T(8,128)} %param.22) | copy-start | bytes 196612
  6.5 66.6 %copy-start.12 = (f32[1024,16]{0,1:T(8,128)S(1)}, f32[1024,16]{0,1:T(8,128)}, u32[]{:S(2)}) copy-start(f32[1024,16]{0,1:T(8,128)} %param.23) | copy-start | bytes 196612
  6.5 140.1 %all-gather.8.cloned.1.call-start = ((), (), s32[]{:S(2)}) async-start(), calls=%async_computation | async-start | bytes 3932160 | tf_op jit(solution)/shard_map/all_gather | solution.py:65
  10.0 95.0 %copy-start.5 = (bf16[512,1024]{1,0:T(8,128)(2,1)S(1)}, bf16[512,1024]{1,0:T(8,128)(2,1)}, u32[]{:S(2)}) copy-start(bf16[512,1024]{1,0:T(8,128)(2,1)} %param.18) | copy-start | bytes 3145732
  10.0 155.1 %all-gather.12.cloned.1.call-start = ((), (), s32[]{:S(2)}) async-start(), calls=%async_computation.2 | async-start | bytes 9437184 | tf_op jit(solution)/shard_map/all_gather | solution.py:78
  10.7 192.7 %all-gather.10.cloned.1.call-start = ((), (), s32[]{:S(2)}) async-start(), calls=%async_computation.1 | async-start | bytes 9437184 | tf_op jit(solution)/shard_map/all_gather | solution.py:77
  11.5 94.8 %copy-start.15 = (bf16[1024]{0:T(1024)(128)(2,1)S(1)}, bf16[1024]{0:T(1024)(128)(2,1)}, u32[]{:S(2)}) copy-start(bf16[1024]{0:T(1024)(128)(2,1)} %param.17) | copy-start | bytes 6148
  11.5 380.5 %all-gather.16.cloned.1.call-start = ((), (), s32[]{:S(2)}) async-start(), calls=%async_computation.4 | async-start | bytes 9437184 | tf_op jit(solution)/shard_map/all_gather | solution.py:132
  11.5 16.1 %collective-permute-start = (bf16[512,1024]{1,0:T(8,128)(2,1)}, bf16[512,1024]{1,0:T(8,128)(2,1)S(1)}, u32[]{:S(2)}, u32[]{:S(2)}) collective-permute-start(bf16[512,1024]{1,0:T(8,128)(2,1)} %param.18), channel_id=1, source_target_pairs={{0,4},{4,8},{8,12},{12,16},{16,20},{20,24},{24,28},{28,0},{1,5},{5... | collective-permute-start | bytes 3145736 | tf_op jit(solution)/shard_map/ppermute | solution.py:17
  27.6 45.5 %copy-start.6 = (bf16[512,1024]{1,0:T(8,128)(2,1)}, bf16[512,1024]{1,0:T(8,128)(2,1)S(1)}, u32[]{:S(2)}) copy-start(bf16[512,1024]{1,0:T(8,128)(2,1)S(1)} %collective-permute-done) | copy-start | bytes 3145732
  27.6 15.1 %collective-permute-start.1 = (bf16[512,1024]{1,0:T(8,128)(2,1)S(1)}, bf16[512,1024]{1,0:T(8,128)(2,1)S(1)}, u32[]{:S(2)}, u32[]{:S(2)}) collective-permute-start(bf16[512,1024]{1,0:T(8,128)(2,1)S(1)} %collective-permute-done), channel_id=1, source_target_pairs={{0,4},{4,8},{8,12},{12,16},{16,20},{20,24},{24,28},{28,0},{1,5},{5... | collective-permute-start | bytes 3145736 | tf_op jit(solution)/shard_map/ppermute | solution.py:17
  42.8 15.1 %copy-start.7 = (bf16[512,1024]{1,0:T(8,128)(2,1)}, bf16[512,1024]{1,0:T(8,128)(2,1)S(1)}, u32[]{:S(2)}) copy-start(bf16[512,1024]{1,0:T(8,128)(2,1)S(1)} %collective-permute-done.1) | copy-start | bytes 3145732
  42.8 15.1 %collective-permute-start.2 = (bf16[512,1024]{1,0:T(8,128)(2,1)S(1)}, bf16[512,1024]{1,0:T(8,128)(2,1)S(1)}, u32[]{:S(2)}, u32[]{:S(2)}) collective-permute-start(bf16[512,1024]{1,0:T(8,128)(2,1)S(1)} %collective-permute-done.1), channel_id=1, source_target_pairs={{0,4},{4,8},{8,12},{12,16},{16,20},{20,24},{24,28},{28,0},{1,5},{5... | collective-permute-start | bytes 3145736 | tf_op jit(solution)/shard_map/ppermute | solution.py:17
  57.9 15.2 %collective-permute-start.3 = (bf16[512,1024]{1,0:T(8,128)(2,1)S(1)}, bf16[512,1024]{1,0:T(8,128)(2,1)}, u32[]{:S(2)}, u32[]{:S(2)}) collective-permute-start(bf16[512,1024]{1,0:T(8,128)(2,1)S(1)} %collective-permute-done.2), channel_id=1, source_target_pairs={{0,4},{4,8},{8,12},{12,16},{16,20},{20,24},{24,28},{28,0},{1,5},{5... | collective-permute-start | bytes 3145736 | tf_op jit(solution)/shard_map/ppermute | solution.py:17
  57.9 397.6 %all-gather.14.cloned.1.call-start = ((), (), s32[]{:S(2)}) async-start(), calls=%async_computation.3 | async-start | bytes 3932160 | tf_op jit(solution)/shard_map/all_gather | solution.py:129
  73.1 32.9 %collective-permute-start.4 = (bf16[512,1024]{1,0:T(8,128)(2,1)}, bf16[512,1024]{1,0:T(8,128)(2,1)}, u32[]{:S(2)}, u32[]{:S(2)}) collective-permute-start(bf16[512,1024]{1,0:T(8,128)(2,1)} %collective-permute-done.3), channel_id=1, source_target_pairs={{0,4},{4,8},{8,12},{12,16},{16,20},{20,24},{24,28},{28,0},{1,5},{5... | collective-permute-start | bytes 3145736 | tf_op jit(solution)/shard_map/ppermute | solution.py:17
  73.2 46.8 %copy-start.13 = (f32[3,3,1024]{2,1,0:T(4,128)S(1)}, f32[3,3,1024]{2,1,0:T(4,128)}, u32[]{:S(2)}) copy-start(f32[3,3,1024]{2,1,0:T(4,128)} %param.21) | copy-start | bytes 110596
  106.0 34.7 %collective-permute-start.5 = (bf16[512,1024]{1,0:T(8,128)(2,1)}, bf16[512,1024]{1,0:T(8,128)(2,1)S(1)}, u32[]{:S(2)}, u32[]{:S(2)}) collective-permute-start(bf16[512,1024]{1,0:T(8,128)(2,1)} %collective-permute-done.4), channel_id=1, source_target_pairs={{0,4},{4,8},{8,12},{12,16},{16,20},{20,24},{24,28},{28,0},{1,5},{5... | collective-permute-start | bytes 3145736 | tf_op jit(solution)/shard_map/ppermute | solution.py:17
  140.8 15.7 %collective-permute-start.6 = (bf16[512,1024]{1,0:T(8,128)(2,1)S(1)}, bf16[512,1024]{1,0:T(8,128)(2,1)}, u32[]{:S(2)}, u32[]{:S(2)}) collective-permute-start(bf16[512,1024]{1,0:T(8,128)(2,1)S(1)} %collective-permute-done.5), channel_id=1, source_target_pairs={{0,4},{4,8},{8,12},{12,16},{16,20},{20,24},{24,28},{28,0},{1,5},{5... | collective-permute-start | bytes 3145736 | tf_op jit(solution)/shard_map/ppermute | solution.py:17
  146.6 12.4 %copy-start.4 = (bf16[384,4096]{1,0:T(8,128)(2,1)S(1)}, bf16[384,4096]{1,0:T(8,128)(2,1)}, u32[]{:S(2)}) copy-start(bf16[384,4096]{1,0:T(8,128)(2,1)} %all-gather.8.cloned.1.call-done) | copy-start | bytes 9437188
  211.2 55.2 %collective-permute-start.7 = (bf16[2,3072]{1,0:T(2,128)(2,1)S(1)}, bf16[2,3072]{1,0:T(2,128)(2,1)S(1)}, u32[]{:S(2)}, u32[]{:S(2)}) collective-permute-start(bf16[2,3072]{1,0:T(2,128)(2,1)S(1)} %pad_maximum_fusion), channel_id=1, source_target_pairs={{0,4},{4,8},{8,12},{12,16},{16,20},{20,24},{24,28},{1,5},{5,9},{9,... | collective-permute-start | bytes 36872 | tf_op jit(solution)/shard_map/ppermute | solution.py:24
  268.5 2.2 copy-start.2
  273.7 19.5 %copy-start.10 = (f32[6,1024,16]{1,2,0:T(8,128)S(1)}, f32[6,1024,16]{1,2,0:T(8,128)}, u32[]{:S(2)}) copy-start(f32[6,1024,16]{1,2,0:T(8,128)} %custom-call.4) | copy-start | bytes 1179652
  316.7 56.2 %copy-start.3 = (f32[6,1024,16]{2,0,1:T(8,128)S(1)}, f32[6,1024,16]{2,0,1:T(8,128)}, u32[]{:S(2)}) copy-start(f32[6,1024,16]{2,0,1:T(8,128)} %copy.38) | copy-start | bytes 1179652
  316.7 56.2 %copy-start.9 = (f32[1024,16]{1,0:T(8,128)S(1)}, f32[1024,16]{1,0:T(8,128)}, u32[]{:S(2)}) copy-start(f32[1024,16]{1,0:T(8,128)} %copy.47) | copy-start | bytes 196612
  372.9 15.2 %copy-start.14 = (f32[1024]{0:T(1024)S(1)}, f32[1024]{0:T(1024)}, u32[]{:S(2)}) copy-start(f32[1024]{0:T(1024)} %param.24) | copy-start | bytes 12292
  385.3 70.2 %copy-start.8 = (bf16[384,1024]{1,0:T(8,128)(2,1)S(1)}, bf16[384,1024]{1,0:T(8,128)(2,1)}, u32[]{:S(2)}) copy-start(bf16[384,1024]{1,0:T(8,128)(2,1)} %convolution_convert_fusion.3) | copy-start | bytes 2359300
  455.5 8.7 %copy-start.1 = (bf16[512,1024]{1,0:T(8,128)(2,1)S(1)}, bf16[512,1024]{1,0:T(8,128)(2,1)}, u32[]{:S(2)}) copy-start(bf16[512,1024]{1,0:T(8,128)(2,1)} %param.16) | copy-start | bytes 3145732
Sparse Core Ops, SparseCore 0:
  10.1 66.1 all-gather.7
  78.2 67.9 all-gather.11
  148.1 55.2 all-gather.9
  205.1 54.2 all-gather.15
  392.1 63.4 all-gather.13
